TPU v7x, 256 devices: a whole 4x4x8 slice. The times are simulated.
256 devices in a mesh: seq: 64 (over z, y, core), tensor: 4 (over x).
Axes of the slice: x: 4, y: 4, z: 8, core: 2. Of those that a mesh axis runs over, the one named last changes fastest.
Arguments:
- tokens: bfloat16 [8192, 1536], P('seq', 'tensor'), may hold values from -6 to 6
- attn_gain: float32 [1536], replicated, may hold values from 0.5 to 1.5
- q_weight: bfloat16 [1536, 1536], P(None, 'tensor'), may hold values from -0.15625 to 0.15625
- key_matrix: bfloat16 [1536, 512], P(None, 'tensor'), may hold values from -0.15625 to 0.15625
- value_matrix: bfloat16 [1536, 512], P(None, 'tensor'), may hold values from -0.15625 to 0.15625
- o_weight: bfloat16 [1536, 1536], P('tensor'), may hold values from -0.625 to 0.625
- moe_gain: float32 [1536], replicated, may hold values from 0.5 to 1.5
- gate_weight: bfloat16 [64, 1536, 512], P('seq', None, 'tensor'), may hold values from -0.15625 to 0.15625
- up_weight: bfloat16 [64, 1536, 512], P('seq', None, 'tensor'), may hold values from -0.15625 to 0.15625
- down_weight: bfloat16 [64, 512, 1536], P('seq', 'tensor'), may hold values from -0.25 to 0.25
- key_page_pool: bfloat16 [4096, 128, 512], P('seq', None, 'tensor'), may hold values from -140 to 140
- value_page_pool: bfloat16 [4096, 128, 512], P('seq', None, 'tensor'), may hold values from -6 to 6
- cache_lens: int32 [64], P('seq'), may hold values from 1 to 8192, as said below
- page_table: int32 [64, 64], P('seq'), may hold values from 0 to 63, each once within a row
- routes: int32 [8192, 8], P('seq'), may hold values from 0 to 39, all different within a row; in each aligned block of 128 rows (0 to 127, 128 to 255, ...) at most 32 rows name the same one
- route_gates: float32 [8192, 8], P('seq'), may hold values from 0.1 to 1
Outputs:
- mixed: bfloat16 [8192, 1536], P('seq', 'tensor')
Inputs may be any that keep to these rules, and one draw needn't show every extreme that they name: `cache_lens`: some request has exactly 8192 cached tokens in every draw. `page_table`: each row is a permutation of 0 .. 63. `routes`: each row names 8 different experts. Among the 128 rows of one request no expert is named more than 32 times, a bound that some block reaches.
All inputs are finite; a program needn't handle non-finite values.
Results may differ from a plain program's by a relative error of at most 0.017.
The roundings to bfloat16 on the way count: a program that leaves them out, or rounds other values in their place, can miss the bound.
Values may be sent and summed in bfloat16 or wider, within the bound.
A program may use at most 128 MiB of HBM per device.

v0:
```python
import jax
import jax.numpy as jnp
from jax import lax
from jax.sharding import PartitionSpec as P

HEAD_SIZE = 64
CAP = 32
NORM_EPSILON = 1e-06
MASKED_SCORE = -1e30


def norm_rows(field, gain_row):
    widened = field.astype(jnp.float32)
    return (
        widened
        * lax.rsqrt(jnp.mean(widened * widened, axis=1, keepdims=True) + NORM_EPSILON)
        * gain_row
    )


def apply_rotary(field, token_places):
    head_dim = field.shape[-1]
    half_dim = head_dim // 2
    frequency = 10000.0 ** (-2.0 * jnp.arange(half_dim, dtype=jnp.float32) / head_dim)
    phase_angle = token_places[:, None, None] * frequency
    cosine = jnp.cos(phase_angle)
    sine_part = jnp.sin(phase_angle)
    lower_half = field[..., :half_dim]
    upper_half = field[..., half_dim:]
    return jnp.concatenate(
        [
            lower_half * cosine - upper_half * sine_part,
            upper_half * cosine + lower_half * sine_part,
        ],
        axis=-1,
    )


def attend(
    query_rows, incoming_keys, incoming_values, key_pool, value_pool, table_row, cached_length
):
    row_count = query_rows.shape[0]
    kv_count = incoming_keys.shape[1]
    head_dim = incoming_keys.shape[2]
    page_count = key_pool.shape[0]
    page_rows = key_pool.shape[1]
    per_block = min(page_count, max(1, 512 // page_rows))
    block_count = page_count // per_block
    block_span = per_block * page_rows
    score_scale = head_dim ** (-0.5)
    causal = jnp.arange(row_count)[None, :] <= jnp.arange(row_count)[:, None]
    fresh_scores = (
        jnp.einsum("tgjd,sgd->gjts", query_rows, incoming_keys, preferred_element_type=jnp.float32)
        * score_scale
    )
    fresh_scores = jnp.where(causal, fresh_scores, MASKED_SCORE)

    def load_block(pool, block_id):
        page_index = lax.dynamic_slice_in_dim(table_row, block_id * per_block, per_block)
        return pool[page_index].reshape(block_span, kv_count, head_dim)

    def weighted(scores, values, row_best):
        weights = jnp.exp(scores - row_best[..., None])
        weights_b = weights.astype(jnp.bfloat16)
        return (
            jnp.sum(weights, axis=-1),
            jnp.einsum("gjts,sgd->gjtd", weights_b, values, preferred_element_type=jnp.float32),
        )

    def block_step(block_id, carried):
        old_best, old_total, old_mix = carried
        block_keys = load_block(key_pool, block_id)
        scores = (
            jnp.einsum("tgjd,sgd->gjts", query_rows, block_keys, preferred_element_type=jnp.float32)
            * score_scale
        )
        visible = block_id * block_span + jnp.arange(block_span, dtype=jnp.int32) < cached_length
        scores = jnp.where(visible, scores, MASKED_SCORE)
        new_best = jnp.maximum(old_best, jnp.max(scores, axis=-1))
        rescale = jnp.exp(old_best - new_best)
        block_total, block_mix = weighted(scores, load_block(value_pool, block_id), new_best)
        return (
            new_best,
            old_total * rescale + block_total,
            old_mix * rescale[..., None] + block_mix,
        )

    first_best = jnp.max(fresh_scores, axis=-1)
    first_total, first_mix = weighted(fresh_scores, incoming_values, first_best)
    _, denominator, mixture = lax.fori_loop(
        0, block_count, block_step, (first_best, first_total, first_mix)
    )
    result = mixture / denominator[..., None]
    return jnp.transpose(result, (2, 0, 1, 3)).reshape(row_count, -1).astype(jnp.bfloat16)


def slot_places(routes, capacity, expert_total):
    flat_routes = routes.reshape(-1)
    route_hits = (
        flat_routes[:, None] == jnp.arange(expert_total, dtype=jnp.int32)[None, :]
    ).astype(jnp.int32)
    earlier = jnp.cumsum(route_hits, axis=0) - route_hits
    return flat_routes * capacity + jnp.sum(earlier * route_hits, axis=1)


def pack_rows(moe_in, slot_place, capacity, expert_total):
    top_count = slot_place.shape[0] // moe_in.shape[0]
    token_rows = jnp.arange(slot_place.shape[0], dtype=jnp.int32) // top_count
    outgoing = jnp.zeros((expert_total * capacity, moe_in.shape[1]), moe_in.dtype)
    outgoing = outgoing.at[slot_place].set(moe_in[token_rows])
    return outgoing.reshape(expert_total, capacity, moe_in.shape[1])


def finish_partial(gate_act, up_act, down_weight, slot_place, route_gates, residual_cols):
    row_count = residual_cols.shape[0]
    hidden = (jax.nn.silu(gate_act) * up_act).astype(jnp.bfloat16)
    expert_out = jnp.einsum(
        "secf,efd->secd", hidden, down_weight, preferred_element_type=jnp.float32
    )
    expert_cols = lax.psum_scatter(
        expert_out.astype(jnp.bfloat16), "tensor", scatter_dimension=3, tiled=True
    )
    col_count = expert_cols.shape[3]
    returned = lax.all_to_all(
        expert_cols.reshape(-1, expert_cols.shape[2], col_count),
        "seq",
        split_axis=0,
        concat_axis=0,
        tiled=True,
    )
    picked = (
        returned.reshape(-1, col_count)[slot_place].astype(jnp.float32)
        * route_gates.reshape(-1)[:, None]
    )
    expert_mix = jnp.sum(picked.reshape(row_count, -1, col_count), axis=1)
    return (residual_cols.astype(jnp.float32) + expert_mix).astype(jnp.bfloat16)


def shards(
    tokens,
    attn_gain,
    q_weight,
    key_matrix,
    value_matrix,
    o_weight,
    moe_gain,
    gate_weight,
    up_weight,
    down_weight,
    key_page_pool,
    value_page_pool,
    cache_lens,
    page_table,
    routes,
    route_gates,
):
    row_count = tokens.shape[0]
    col_count = tokens.shape[1]
    group_count = lax.axis_size("seq")
    tensor_index = lax.axis_index("tensor")
    column_start = tensor_index * col_count
    local_experts = gate_weight.shape[0]
    expert_total = local_experts * group_count
    whole = lax.all_gather(tokens, "tensor", axis=1, tiled=True)
    normed = norm_rows(whole, attn_gain).astype(jnp.bfloat16)
    head_count = q_weight.shape[1] // HEAD_SIZE
    kv_count = key_matrix.shape[1] // HEAD_SIZE
    token_places = (cache_lens[0] + jnp.arange(row_count, dtype=jnp.int32)).astype(jnp.float32)
    query_rows = jnp.dot(normed, q_weight, preferred_element_type=jnp.float32).reshape(
        row_count, head_count, HEAD_SIZE
    )
    query_rows = (
        apply_rotary(query_rows, token_places)
        .astype(jnp.bfloat16)
        .reshape(row_count, kv_count, head_count // kv_count, HEAD_SIZE)
    )
    incoming_keys = jnp.dot(normed, key_matrix, preferred_element_type=jnp.float32).reshape(
        row_count, kv_count, HEAD_SIZE
    )
    incoming_keys = apply_rotary(incoming_keys, token_places).astype(jnp.bfloat16)
    incoming_values = (
        jnp.dot(normed, value_matrix, preferred_element_type=jnp.float32)
        .reshape(row_count, kv_count, HEAD_SIZE)
        .astype(jnp.bfloat16)
    )
    attended = attend(
        query_rows,
        incoming_keys,
        incoming_values,
        key_page_pool,
        value_page_pool,
        page_table[0],
        cache_lens[0],
    )
    partial_value = jnp.dot(attended, o_weight, preferred_element_type=jnp.float32)
    slot_place = slot_places(routes, CAP, expert_total)
    summed = lax.psum(partial_value.astype(jnp.bfloat16), "tensor").astype(jnp.float32)
    residual = (whole.astype(jnp.float32) + summed).astype(jnp.bfloat16)
    moe_in = norm_rows(residual, moe_gain).astype(jnp.bfloat16)
    residual_cols = lax.dynamic_slice_in_dim(residual, column_start, col_count, 1)
    received = lax.all_to_all(
        pack_rows(moe_in, slot_place, CAP, expert_total),
        "seq",
        split_axis=0,
        concat_axis=0,
        tiled=True,
    )
    received = received.reshape(group_count, local_experts, CAP, -1)
    gate_act = jnp.einsum(
        "secd,edf->secf", received, gate_weight, preferred_element_type=jnp.float32
    )
    up_act = jnp.einsum("secd,edf->secf", received, up_weight, preferred_element_type=jnp.float32)
    return finish_partial(gate_act, up_act, down_weight, slot_place, route_gates, residual_cols)


def solution(mesh):
    in_specs = (
        P("seq", "tensor"),
        P(),
        P(None, "tensor"),
        P(None, "tensor"),
        P(None, "tensor"),
        P("tensor", None),
        P(),
        P("seq", None, "tensor"),
        P("seq", None, "tensor"),
        P("seq", "tensor", None),
        P("seq", None, "tensor"),
        P("seq", None, "tensor"),
        P("seq"),
        P("seq", None),
        P("seq", None),
        P("seq", None),
    )
    out_specs = P("seq", "tensor")
    return jax.shard_map(shards, mesh=mesh, in_specs=in_specs, out_specs=out_specs, check_vma=False)
```

profile of v0, /device:TPU:1, one launch (start us, length us, event | category | flops | bytes accessed | tf_op | source)
XLA Modules:
  0.0 581.9 jit_solution(12883326083600127530)
XLA Ops:
  6.6 12.0 %all_gather.3 = bf16[128,1536]{1,0:T(8,128)(2,1)S(1)} all-gather(bf16[128,384]{1,0:T(8,128)(2,1)} %param.18), channel_id=1, replica_groups=mesh['seq'=64,'tensor'=4] {'tensor'}, dimensions={1}, use_global_device_ids=true | all-gather | bytes 491520 | tf_op jit(solution)/shard_map/all_gather | solution.py:164
  23.0 106.6 %while.17 = (s32[]{:T(128)}, f32[2,3,128]{2,1,0:T(4,128)S(1)}, f32[2,3,128]{2,1,0:T(4,128)S(1)}, f32[2,3,128,64]{2,3,1,0:T(8,128)S(1)}, s32[]{:T(128)}, /*index=...) while((s32[]{:T(128)}, f32[2,3,128]{2,1,0:T(4,128)S(1)}, ...), condition=%wide.region_6.7_spmd, body=%wide.region_3.6_spmd.sunk | while | flops 103517712 | bytes 7099675 | solution.py:90
  26.8 2.2 gather_fusion.1
  33.5 2.2 gather_fusion.1
  40.1 2.2 gather_fusion.1
  46.8 2.2 gather_fusion.1
  53.5 2.2 gather_fusion.1
  60.1 2.2 gather_fusion.1
  66.8 2.2 gather_fusion.1
  73.5 2.2 gather_fusion.1
  80.1 2.2 gather_fusion.1
  86.8 2.2 gather_fusion.1
  93.4 2.2 gather_fusion.1
  100.1 2.2 gather_fusion.1
  106.8 2.2 gather_fusion.1
  113.4 2.2 gather_fusion.1
  120.1 2.2 gather_fusion.1
  126.7 2.2 gather_fusion.1
  131.3 18.0 %reduce-window.6 = s32[64,8,128]{2,1,0:T(8,128)S(1)} reduce-window(s32[64,8,128]{2,1,0:T(8,128)S(1)} %fusion.33, s32[]{:T(128)} %constant.103.clone.1), window={size=1x1x128 pad=0_0x0_0x127_0}, to_apply=%region_8.9 | reduce-window | flops 8323072 | bytes 524292 | tf_op jit(solution)/shard_map/reduce-window
  150.2 30.9 %all-reduce.2.cloned.1.call-done = bf16[128,1536]{1,0:T(8,128)(2,1)} async-done(((bf16[128,1536]{1,0:T(8,128)(2,1)}), bf16[128,1536]{1,0:T(8,128)(2,1)}) %all-reduce.2.cloned.1.call-update) | async-done | bytes 393232 | tf_op jit(solution)/shard_map/psum | solution.py:197
  182.6 19.7 %scatter_custom_fusion = bf16[2048,1536]{1,0:T(8,128)(2,1)} fusion(s32[1024]{0:T(1024)S(1)} %bitcast.160, bf16[128,1536]{1,0:T(8,128)(2,1)S(1)} %fusion.18, s32[1024]{0:T(1024)S(1)} %broadcast_clamp_fusion.1, bf16[]{:T(256)} %constant.115.clone.1), kind=kCustom, calls=%fused_computation.21 | custom fusion | bytes 6291458 | tf_op jit(solution)/shard_map/scatter | solution.py:110
  202.3 152.4 %all_to_all.10 = bf16[64,32,1536]{2,1,0:T(8,128)(2,1)S(1)} all-to-all(bf16[64,32,1536]{2,1,0:T(8,128)(2,1)} %bitcast.146), channel_id=1, replica_groups=mesh['seq'=64,'tensor'=4] {'seq'}, dimensions={0} | all-to-all | bytes 12582912 | tf_op jit(solution)/shard_map/all_to_all | solution.py:201
  354.7 2.7 copy-done.2
  359.2 11.8 %convert_bitcast_fusion = bf16[64,1,32,1536]{3,2,0,1:T(8,128)(2,1)} fusion(bf16[64,32,1536]{2,1,0:T(8,128)(2,1)} %copy-done.2, f32[64,1,32,128]{3,2,0,1:T(8,128)S(1)} %convolution_bitcast_fusion.1, bf16[1,128,1536]{2,1,0:T(8,128)(2,1)S(1)} %copy-done.6, bf16[1,1536,128]{2,1,0:T(8,128)(2,1)S(1)} %copy-done.7), kind=kOutput, calls=%fused_computation.20 | convolution fusion | flops 1615331328 | bytes 14417920 | tf_op jit(solution)/shard_map/secf,efd->secd/dot_general | solution.py:117
  371.0 33.7 %copy.55 = bf16[64,1,32,1536]{2,0,1,3:T(8,128)(2,1)} copy(bf16[64,1,32,1536]{3,2,0,1:T(8,128)(2,1)} %convert_bitcast_fusion) | data formatting | bytes 12582912
  404.7 33.1 %reshape.310 = bf16[1536,2048]{1,0:T(8,128)(2,1)} reshape(bf16[1536,1,64,32]{3,2,1,0:T(8,128)(2,1)} %bitcast.144) | data formatting | bytes 12582912
  437.8 63.6 %reduce-scatter.4.cloned.1.call-done = bf16[384,2048]{1,0:T(8,128)(2,1)} async-done(((bf16[1536,2048]{1,0:T(8,128)(2,1)}), bf16[384,2048]{1,0:T(8,128)(2,1)}) %reduce-scatter.4.cloned.1.call-update) | async-done | bytes 1572880
  501.4 8.4 %reshape.311 = bf16[384,1,64,32]{3,2,1,0:T(8,128)(2,1)} reshape(bf16[384,2048]{1,0:T(8,128)(2,1)} %reduce-scatter.4.cloned.1.call-done) | data formatting | bytes 3145728
  509.7 8.7 %copy.56 = bf16[64,1,32,384]{3,2,0,1:T(8,128)(2,1)} copy(bf16[64,1,32,384]{2,0,1,3:T(8,128)(2,1)} %bitcast.147) | data formatting | bytes 3145728
  518.5 10.8 %all-to-all-start.1 = ((bf16[64,32,384]{2,1,0:T(8,128)(2,1)}), bf16[64,32,384]{2,1,0:T(8,128)(2,1)S(1)}, u32[]{:S(2)}, u32[]{:S(2)}) async-start(bf16[64,32,384]{2,1,0:T(8,128)(2,1)} %bitcast.148), calls=%async_computation.1 | async-start | bytes 3145728 | tf_op jit(solution)/shard_map/all_to_all | solution.py:124
  530.0 38.2 %all-to-all-done.1 = bf16[64,32,384]{2,1,0:T(8,128)(2,1)S(1)} async-done(((bf16[64,32,384]{2,1,0:T(8,128)(2,1)}), bf16[64,32,384]{2,1,0:T(8,128)(2,1)S(1)}, u32[]{:S(2)}, u32[]{:S(2)}) %all-to-all-start.1) | async-done | bytes 1572896 | tf_op jit(solution)/shard_map/all_to_all | solution.py:124
  568.2 3.9 gather_fusion.2
  (301 shorter events, 83.3 us)
Async XLA Ops:
  6.5 123.1 %copy-start = (bf16[384,1536]{1,0:T(8,128)(2,1)S(1)}, bf16[384,1536]{1,0:T(8,128)(2,1)}, u32[]{:S(2)}) copy-start(bf16[384,1536]{1,0:T(8,128)(2,1)} %param.23) | copy-start | bytes 3538948
  6.5 14.9 %copy-start.9 = (f32[1536]{0:T(1024)S(1)}, f32[1536]{0:T(1024)}, u32[]{:S(2)}) copy-start(f32[1536]{0:T(1024)} %param.19) | copy-start | bytes 18436
  6.5 14.9 %copy-start.12 = (bf16[1536,128]{1,0:T(8,128)(2,1)S(1)}, bf16[1536,128]{1,0:T(8,128)(2,1)}, u32[]{:S(2)}) copy-start(bf16[1536,128]{1,0:T(8,128)(2,1)} %param.21) | copy-start | bytes 1179652
  6.5 15.5 %copy-start.13 = (bf16[1536,128]{1,0:T(8,128)(2,1)S(1)}, bf16[1536,128]{1,0:T(8,128)(2,1)}, u32[]{:S(2)}) copy-start(bf16[1536,128]{1,0:T(8,128)(2,1)} %param.22) | copy-start | bytes 1179652
  6.5 174.6 %all-reduce.2.cloned.1.call-start = ((), (), s32[]{:S(2)}) async-start(), calls=%async_computation.3 | async-start | bytes 786432 | tf_op jit(solution)/shard_map/psum | solution.py:197
  18.7 3.7 copy-start.3
  21.4 1.5 copy-start.15
  129.6 1.5 copy-start.8
  129.6 51.6 %copy-start.4 = (bf16[128,1536]{1,0:T(8,128)(2,1)S(1)}, bf16[128,1536]{1,0:T(8,128)(2,1)}, u32[]{:S(2)}) copy-start(bf16[128,1536]{1,0:T(8,128)(2,1)} %copy-done.3) | copy-start | bytes 1179652
  130.8 51.6 %copy-start.10 = (f32[1536]{0:T(1024)S(1)}, f32[1536]{0:T(1024)}, u32[]{:S(2)}) copy-start(f32[1536]{0:T(1024)} %param.24) | copy-start | bytes 18436
  130.8 370.6 %reduce-scatter.4.cloned.1.call-start = ((), (), s32[]{:S(2)}) async-start(), calls=%async_computation.4 | async-start | bytes 7864320
  182.4 19.9 %copy-start.5 = (bf16[128,1536]{1,0:T(8,128)(2,1)}, bf16[128,1536]{1,0:T(8,128)(2,1)S(1)}, u32[]{:S(2)}) copy-start(bf16[128,1536]{1,0:T(8,128)(2,1)S(1)} %get-tuple-element.183) | copy-start | bytes 1179652
  202.3 155.0 %copy-start.14 = (bf16[1,1536,128]{2,1,0:T(8,128)(2,1)S(1)}, bf16[1,1536,128]{2,1,0:T(8,128)(2,1)}, u32[]{:S(2)}) copy-start(bf16[1,1536,128]{2,1,0:T(8,128)(2,1)} %param.25) | copy-start | bytes 1179652
  354.7 2.7 copy-start.2
  357.4 1.8 copy-start.6
  357.4 1.8 copy-start.7
  518.5 10.8 %copy-start.11 = (f32[128,8]{0,1:T(8,128)S(1)}, f32[128,8]{0,1:T(8,128)}, u32[]{:S(2)}) copy-start(f32[128,8]{0,1:T(8,128)} %param.33) | copy-start | bytes 12292
  518.5 49.8 %all-to-all-start.1 = ((bf16[64,32,384]{2,1,0:T(8,128)(2,1)}), bf16[64,32,384]{2,1,0:T(8,128)(2,1)S(1)}, u32[]{:S(2)}, u32[]{:S(2)}) async-start(bf16[64,32,384]{2,1,0:T(8,128)(2,1)} %bitcast.148), calls=%async_computation.1 | async-start | bytes 3145728 | tf_op jit(solution)/shard_map/all_to_all | solution.py:124
  568.2 6.9 %copy-start.1 = (bf16[384,1536]{1,0:T(8,128)(2,1)S(1)}, bf16[384,1536]{1,0:T(8,128)(2,1)}, u32[]{:S(2)}) copy-start(bf16[384,1536]{1,0:T(8,128)(2,1)} %param.23) | copy-start | bytes 3538948
Sparse Core Ops, SparseCore 0:
  130.9 50.2 all-reduce.1
  437.9 63.4 reduce-scatter.3
where the time goes:
time: 585 us; the launch traced here: 582 us
  local copies, waits for them, and re-layouts  187 us (32%)
  blocking collectives  164 us (28%)
  waiting for transfers between devices  133 us (23%)
  other arithmetic  38.9 us (7%)
  matrix products  31.2 us (5%)
  between operations  14.4 us (2%)
  starting transfers between devices  11 us (2%)
    all_to_all x1, blocking collectives, shards(): lax.all_to_all(pack_rows(moe_in, slot_place, CAP, expert_total), 'seq', s...  152 us
    unnamed x38, local copies, waits for them, and re-layouts  87.4 us
    gather x64, local copies, waits for them, and re-layouts, load_block(): return pool[page_index].reshape(block_span, kv_count, head_dim)  73.8 us
    unnamed x3, waiting for transfers between devices  63.6 us
    all_to_all x1, waiting for transfers between devices, finish_partial(): lax.all_to_all(expert_cols.reshape(-1, expert_cols.shape[2], col_count),...  38.2 us
    psum x1, waiting for transfers between devices, shards(): lax.psum(partial_value.astype(jnp.bfloat16), 'tensor').astype(jnp.float32)  30.9 us
    scatter x1, local copies, waits for them, and re-layouts, pack_rows(): outgoing = outgoing.at[slot_place].set(moe_in[token_rows])  19.7 us
    another operation x5, other arithmetic  18.2 us
  transfers between devices with their start and end apart: 3, of which 3 were waited for; matrix products, arithmetic and copies ran while one was open for 3% of the time, Pallas kernels for 0%

commit v1 on v0

--- a/solution.py
+++ b/solution.py
@@ -161,7 +161,8 @@
     column_start = tensor_index * col_count
     local_experts = gate_weight.shape[0]
     expert_total = local_experts * group_count
-    whole = lax.all_gather(tokens, "tensor", axis=1, tiled=True)
+    copies = jnp.concatenate([tokens] * lax.axis_size("tensor"), axis=1)
+    whole = lax.all_to_all(copies, "tensor", 1, 1, tiled=True)
     normed = norm_rows(whole, attn_gain).astype(jnp.bfloat16)
     head_count = q_weight.shape[1] // HEAD_SIZE
     kv_count = key_matrix.shape[1] // HEAD_SIZE

time: 585 us -> 633 us (1.082)
  other arithmetic: 38.9 us -> 67.1 us
  waiting for transfers between devices: 133 us -> 150 us
  blocking collectives: 164 us -> 153 us
  local copies, waits for them, and re-layouts: 187 us -> 197 us
    psum x1, waiting for transfers between devices: 30.9 us -> 48.3 us  [shards(): lax.psum(partial_value.astype(jnp.bfloat16), 'tensor').astype(jnp.float32)]
    another operation x5, other arithmetic: 18.2 us -> 31.8 us
    all_gather x1 -> x0, blocking collectives: 12 us -> none  [shards(): whole = lax.all_gather(tokens, 'tensor', axis=1, tiled=True)]
    select_n x16, other arithmetic: 1.25 us -> 11.7 us  [load_block(): return pool[page_index].reshape(block_span, kv_count, head_dim)]
    unnamed x38 -> x52, local copies, waits for them, and re-layouts: 87.4 us -> 93.4 us
  transfers between devices with their start and end apart: 3 -> 4, of which waited for: 3 -> 3; matrix products, arithmetic and copies ran while one was open for 3% -> 7% of each run, Pallas kernels for 0% -> 0%
where the time goes in v1:
time: 633 us; the launch traced here: 628 us
  local copies, waits for them, and re-layouts  197 us (31%)
  blocking collectives  153 us (24%)
  waiting for transfers between devices  150 us (24%)
  other arithmetic  67.1 us (11%)
  matrix products  29.5 us (5%)
  starting transfers between devices  15.8 us (2%)
  between operations  14.4 us (2%)
    all_to_all x1, blocking collectives, shards(): lax.all_to_all(pack_rows(moe_in, slot_place, CAP, expert_total), 'seq', s...  153 us
    unnamed x52, local copies, waits for them, and re-layouts  93.4 us
    gather x64, local copies, waits for them, and re-layouts, load_block(): return pool[page_index].reshape(block_span, kv_count, head_dim)  73.7 us
    unnamed x3, waiting for transfers between devices  63.6 us
    psum x1, waiting for transfers between devices, shards(): lax.psum(partial_value.astype(jnp.bfloat16), 'tensor').astype(jnp.float32)  48.3 us
    all_to_all x1, waiting for transfers between devices, finish_partial(): lax.all_to_all(expert_cols.reshape(-1, expert_cols.shape[2], col_count),...  38.2 us
    another operation x5, other arithmetic  31.8 us
    scatter x1, local copies, waits for them, and re-layouts, pack_rows(): outgoing = outgoing.at[slot_place].set(moe_in[token_rows])  19.7 us
  transfers between devices with their start and end apart: 4, of which 3 were waited for; matrix products, arithmetic and copies ran while one was open for 7% of the time, Pallas kernels for 0%

profile of v1, /device:TPU:1, one launch (start us, length us, event | category | flops | bytes accessed | tf_op | source)
XLA Modules:
  0.0 628.4 jit_solution(3404275839200070242)
XLA Ops:
  8.6 4.8 all-to-all-start
  21.5 30.9 %reduce-window.6 = s32[64,8,128]{2,1,0:T(8,128)S(1)} reduce-window(s32[64,8,128]{2,1,0:T(8,128)} %fusion.31, s32[]{:T(128)} %constant.103.clone.1), window={size=1x1x128 pad=0_0x0_0x127_0}, to_apply=%region_8.9 | reduce-window | flops 8323072 | bytes 524292 | tf_op jit(solution)/shard_map/reduce-window
  60.0 117.1 %while.17 = (s32[]{:T(128)}, f32[2,3,128]{2,1,0:T(4,128)S(1)}, f32[2,3,128]{2,1,0:T(4,128)S(1)}, f32[2,3,128,64]{2,3,1,0:T(8,128)S(1)}, s32[]{:T(128)}, /*index=...) while((s32[]{:T(128)}, f32[2,3,128]{2,1,0:T(4,128)S(1)}, ...), condition=%wide.region_6.7_spmd, body=%wide.region_3.6_spmd.sunk | while | flops 103517712 | bytes 7099675 | solution.py:90
  64.5 2.2 gather_fusion.1
  71.8 2.2 gather_fusion.1
  79.1 2.2 gather_fusion.1
  86.4 2.2 gather_fusion.1
  93.7 2.2 gather_fusion.1
  101.0 2.2 gather_fusion.1
  108.4 2.2 gather_fusion.1
  115.7 2.2 gather_fusion.1
  123.0 2.2 gather_fusion.1
  130.3 2.2 gather_fusion.1
  137.6 2.2 gather_fusion.1
  145.0 2.2 gather_fusion.1
  152.3 2.2 gather_fusion.1
  159.6 2.2 gather_fusion.1
  166.9 2.2 gather_fusion.1
  174.2 2.2 gather_fusion.1
  179.1 48.3 %all-reduce.2.cloned.1.call-done = bf16[128,1536]{1,0:T(8,128)(2,1)} async-done(((bf16[128,1536]{1,0:T(8,128)(2,1)}), bf16[128,1536]{1,0:T(8,128)(2,1)}) %all-reduce.2.cloned.1.call-update) | async-done | bytes 393232 | tf_op jit(solution)/shard_map/psum | solution.py:198
  228.9 19.7 %scatter_custom_fusion = bf16[2048,1536]{1,0:T(8,128)(2,1)} fusion(s32[1024]{0:T(1024)S(1)} %bitcast.183, bf16[128,1536]{1,0:T(8,128)(2,1)S(1)} %fusion.19, s32[1024]{0:T(1024)S(1)} %broadcast_clamp_fusion.1, bf16[]{:T(256)} %constant.115.clone.1), kind=kCustom, calls=%fused_computation.21 | custom fusion | bytes 6291458 | tf_op jit(solution)/shard_map/scatter | solution.py:110
  248.6 152.6 %all_to_all.19 = bf16[64,32,1536]{2,1,0:T(8,128)(2,1)S(1)} all-to-all(bf16[64,32,1536]{2,1,0:T(8,128)(2,1)} %bitcast.164), channel_id=1, replica_groups=mesh['seq'=64,'tensor'=4] {'seq'}, dimensions={0} | all-to-all | bytes 12582912 | tf_op jit(solution)/shard_map/all_to_all | solution.py:202
  401.2 2.6 copy-done.2
  405.7 11.8 %convert_bitcast_fusion = bf16[64,1,32,1536]{3,2,0,1:T(8,128)(2,1)} fusion(bf16[64,32,1536]{2,1,0:T(8,128)(2,1)} %copy-done.2, f32[64,1,32,128]{3,2,0,1:T(8,128)S(1)} %convolution_bitcast_fusion.1, bf16[1,128,1536]{2,1,0:T(8,128)(2,1)S(1)} %copy-done.10, bf16[1,1536,128]{2,1,0:T(8,128)(2,1)S(1)} %copy-done.11), kind=kOutput, calls=%fused_computation.20 | convolution fusion | flops 1615331328 | bytes 14417920 | tf_op jit(solution)/shard_map/secf,efd->secd/dot_general | solution.py:117
  417.5 33.7 %copy.87 = bf16[64,1,32,1536]{2,0,1,3:T(8,128)(2,1)} copy(bf16[64,1,32,1536]{3,2,0,1:T(8,128)(2,1)} %convert_bitcast_fusion) | data formatting | bytes 12582912
  451.1 33.1 %reshape.345 = bf16[1536,2048]{1,0:T(8,128)(2,1)} reshape(bf16[1536,1,64,32]{3,2,1,0:T(8,128)(2,1)} %bitcast.162) | data formatting | bytes 12582912
  484.2 63.6 %reduce-scatter.4.cloned.1.call-done = bf16[384,2048]{1,0:T(8,128)(2,1)} async-done(((bf16[1536,2048]{1,0:T(8,128)(2,1)}), bf16[384,2048]{1,0:T(8,128)(2,1)}) %reduce-scatter.4.cloned.1.call-update) | async-done | bytes 1572880
  547.8 8.4 %reshape.346 = bf16[384,1,64,32]{3,2,1,0:T(8,128)(2,1)} reshape(bf16[384,2048]{1,0:T(8,128)(2,1)} %reduce-scatter.4.cloned.1.call-done) | data formatting | bytes 3145728
  556.2 8.7 %copy.88 = bf16[64,1,32,384]{3,2,0,1:T(8,128)(2,1)} copy(bf16[64,1,32,384]{2,0,1,3:T(8,128)(2,1)} %bitcast.165) | data formatting | bytes 3145728
  564.9 10.8 %all-to-all-start.2 = ((bf16[64,32,384]{2,1,0:T(8,128)(2,1)}), bf16[64,32,384]{2,1,0:T(8,128)(2,1)S(1)}, u32[]{:S(2)}, u32[]{:S(2)}) async-start(bf16[64,32,384]{2,1,0:T(8,128)(2,1)} %bitcast.170), calls=%async_computation.2 | async-start | bytes 3145728 | tf_op jit(solution)/shard_map/all_to_all | solution.py:124
  576.4 38.2 %all-to-all-done.2 = bf16[64,32,384]{2,1,0:T(8,128)(2,1)S(1)} async-done(((bf16[64,32,384]{2,1,0:T(8,128)(2,1)}), bf16[64,32,384]{2,1,0:T(8,128)(2,1)S(1)}, u32[]{:S(2)}, u32[]{:S(2)}) %all-to-all-start.2) | async-done | bytes 1572896 | tf_op jit(solution)/shard_map/all_to_all | solution.py:124
  614.7 3.9 gather_fusion.2
  (321 shorter events, 106.5 us)
Async XLA Ops:
  6.5 170.6 %copy-start = (bf16[384,1536]{1,0:T(8,128)(2,1)S(1)}, bf16[384,1536]{1,0:T(8,128)(2,1)}, u32[]{:S(2)}) copy-start(bf16[384,1536]{1,0:T(8,128)(2,1)} %param.23) | copy-start | bytes 3538948
  6.5 7.5 %copy-start.13 = (s32[128,8]{0,1:T(8,128)S(1)}, s32[128,8]{0,1:T(8,128)}, u32[]{:S(2)}) copy-start(s32[128,8]{0,1:T(8,128)} %param.32) | copy-start | bytes 12292
  6.5 8.3 %copy-start.18 = (f32[1536]{0:T(1024)S(1)}, f32[1536]{0:T(1024)}, u32[]{:S(2)}) copy-start(f32[1536]{0:T(1024)} %param.19) | copy-start | bytes 18436
  8.6 48.0 %all-to-all-start = ((bf16[128,4,384]{2,0,1:T(8,128)(2,1)}), bf16[128,4,384]{2,0,1:T(8,128)(2,1)S(1)}, u32[]{:S(2)}, u32[]{:S(2)}) async-start(bf16[128,4,384]{2,0,1:T(8,128)(2,1)} %copy.58), calls=%async_computation | async-start | bytes 786432 | tf_op jit(solution)/shard_map/all_to_all | solution.py:165
  13.5 214.0 %all-reduce.2.cloned.1.call-start = ((), (), s32[]{:S(2)}) async-start(), calls=%async_computation.4 | async-start | bytes 786432 | tf_op jit(solution)/shard_map/psum | solution.py:198
  14.2 6.6 %copy-start.8 = (s32[128,8]{1,0:T(8,128)}, s32[128,8]{1,0:T(8,128)S(1)}, u32[]{:S(2)}) copy-start(s32[128,8]{1,0:T(8,128)S(1)} %copy.69) | copy-start | bytes 12292
  56.9 2.0 copy-start.3
  56.9 2.0 copy-start.12
  57.1 1.8 copy-start.15
  58.6 1.0 copy-start.6
  177.0 1.5 copy-start.16
  177.0 1.5 copy-start.9
  177.1 1.6 copy-start.14
  177.1 1.8 copy-start.7
  177.1 1.9 copy-start.4
  178.3 50.4 %copy-start.17 = (f32[1536]{0:T(1024)S(1)}, f32[1536]{0:T(1024)}, u32[]{:S(2)}) copy-start(f32[1536]{0:T(1024)} %param.24) | copy-start | bytes 18436
  178.3 369.5 %reduce-scatter.4.cloned.1.call-start = ((), (), s32[]{:S(2)}) async-start(), calls=%async_computation.5 | async-start | bytes 7864320
  228.7 19.9 %copy-start.5 = (bf16[128,1536]{1,0:T(8,128)(2,1)}, bf16[128,1536]{1,0:T(8,128)(2,1)S(1)}, u32[]{:S(2)}) copy-start(bf16[128,1536]{1,0:T(8,128)(2,1)S(1)} %get-tuple-element.183) | copy-start | bytes 1179652
  248.6 155.2 %copy-start.20 = (bf16[1,1536,128]{2,1,0:T(8,128)(2,1)S(1)}, bf16[1,1536,128]{2,1,0:T(8,128)(2,1)}, u32[]{:S(2)}) copy-start(bf16[1,1536,128]{2,1,0:T(8,128)(2,1)} %param.25) | copy-start | bytes 1179652
  401.2 2.7 copy-start.2
  403.8 1.8 copy-start.10
  403.8 1.9 copy-start.11
  564.9 10.8 %copy-start.19 = (f32[128,8]{0,1:T(8,128)S(1)}, f32[128,8]{0,1:T(8,128)}, u32[]{:S(2)}) copy-start(f32[128,8]{0,1:T(8,128)} %param.33) | copy-start | bytes 12292
  564.9 49.8 %all-to-all-start.2 = ((bf16[64,32,384]{2,1,0:T(8,128)(2,1)}), bf16[64,32,384]{2,1,0:T(8,128)(2,1)S(1)}, u32[]{:S(2)}, u32[]{:S(2)}) async-start(bf16[64,32,384]{2,1,0:T(8,128)(2,1)} %bitcast.170), calls=%async_computation.2 | async-start | bytes 3145728 | tf_op jit(solution)/shard_map/all_to_all | solution.py:124
  614.7 6.9 %copy-start.1 = (bf16[384,1536]{1,0:T(8,128)(2,1)S(1)}, bf16[384,1536]{1,0:T(8,128)(2,1)}, u32[]{:S(2)}) copy-start(bf16[384,1536]{1,0:T(8,128)(2,1)} %param.23) | copy-start | bytes 3538948
Sparse Core Ops, SparseCore 0:
  178.4 49.0 all-reduce.1
  484.3 63.4 reduce-scatter.3
